TPU v7x, 512 devices: a whole 4x8x8 slice. The times are simulated.
512 devices in a mesh: grp: 16 (over y, x_hi), blk: 32 (over x_lo, z, core).
Axes of the slice: x: 4 (x_hi: 2, x_lo: 2; x = x_hi * 2 + x_lo), y: 8, z: 8, core: 2. Of those that a mesh axis runs over, the one named last changes fastest.
Arguments:
- sigma_anc: float32 [16384, 16384], P('grp', 'blk')
- panels: float32 [16384, 1024], P(('grp', 'blk')), may hold values from -0.0625 to 0.0625
- diag_inv: float32 [1024, 256], replicated, may hold values from -6 to 6
- scaled_parent_panel: float32 [512, 256], replicated, may hold values from -0.375 to 0.375
- struct_upper: int32 [2, 32], replicated, may hold values from 0 to 63, as said below
- struct_lower: int32 [2, 16], replicated, may hold values from 0 to 63, as said below
Outputs:
- cov_panel: float32 [16384, 1024], P(('blk', 'grp'))
- cov_diag: float32 [1024, 256], P('blk')
- cov_parent: float32 [512, 256], P('blk')
Inputs may be any that keep to these rules, and one draw needn't show every extreme that they name: `struct_upper`: each row lists 32 different ancestor blocks. `struct_lower`: each row lists 16 different blocks, all in its parent's row of struct_upper.
All inputs are finite; a program needn't handle non-finite values.
Results may differ from a plain program's by a relative error of at most 0.00011.
Values sent between devices are 32-bit elements; how exact they have to be, the bound alone decides.
A program may use at most 64 MiB of HBM per device.

v0:
```python
import jax
import jax.numpy as jnp
from jax import lax
from jax.sharding import PartitionSpec as P

NODE_WIDTH = 256
UPPER_NODES_1 = 2
LOWER_NODES_2 = 2
HIGH_ACCURACY = lax.Precision.HIGHEST


def block_table(struct_upper, struct_lower, blocks):
    ids = jnp.arange(blocks, dtype=jnp.int32)
    upper = jnp.any(struct_upper[:, :, None] == ids[None, None, :], axis=1)
    lower = jnp.any(struct_lower[:, :, None] == ids[None, None, :], axis=1)
    return jnp.concatenate([upper, lower], axis=0).astype(jnp.float32)


def row_mask(table, first_row, count):
    blocks = table.shape[1]
    rows = first_row + jnp.arange(count, dtype=jnp.int32)
    membership_grid = (
        (rows // NODE_WIDTH)[:, None] == jnp.arange(blocks, dtype=jnp.int32)[None, :]
    ).astype(jnp.float32)
    return jnp.dot(
        membership_grid, table.T, precision=HIGH_ACCURACY, preferred_element_type=jnp.float32
    )


def strip_summands(reciprocal_lines, array_lines, membership_grid, stacked_arrays):
    count = reciprocal_lines.shape[0]
    upper_width_1 = UPPER_NODES_1 * NODE_WIDTH
    matrix_columns = jnp.repeat(array_lines, NODE_WIDTH, axis=1)
    g_up = -(matrix_columns[:, :upper_width_1] * reciprocal_lines[:, :upper_width_1])
    collected_elder_share = jnp.einsum(
        "rjw,cj->rcw",
        g_up.reshape(count, UPPER_NODES_1, NODE_WIDTH),
        membership_grid,
        precision=HIGH_ACCURACY,
    )
    resolved_bottom_share = matrix_columns[:, upper_width_1:].reshape(
        count, LOWER_NODES_2, NODE_WIDTH
    ) * (
        jnp.einsum("odf,dfy->ody", collected_elder_share, stacked_arrays, precision=HIGH_ACCURACY)
        + reciprocal_lines[:, upper_width_1:].reshape(count, LOWER_NODES_2, NODE_WIDTH)
    )
    strip_result = jnp.concatenate(
        [g_up, -resolved_bottom_share.reshape(count, LOWER_NODES_2 * NODE_WIDTH)], axis=1
    )
    return (strip_result, collected_elder_share, resolved_bottom_share)


def block_sums(urows, reciprocal_lines, collected_elder_share, resolved_bottom_share):
    count = urows.shape[0]
    upper_width_1 = UPPER_NODES_1 * NODE_WIDTH
    u_up = urows[:, :upper_width_1].reshape(count, UPPER_NODES_1, NODE_WIDTH)
    u_low = urows[:, upper_width_1:].reshape(count, LOWER_NODES_2, NODE_WIDTH)
    amat = jnp.einsum(
        "rjw,rjv->jwv",
        u_up,
        reciprocal_lines[:, :upper_width_1].reshape(count, UPPER_NODES_1, NODE_WIDTH),
        precision=HIGH_ACCURACY,
    )
    block_matrix = jnp.einsum("rcw,rcv->cwv", u_low, collected_elder_share, precision=HIGH_ACCURACY)
    extra_matrix = jnp.einsum("rcw,rcv->cwv", u_low, resolved_bottom_share, precision=HIGH_ACCURACY)
    return jnp.concatenate([amat, block_matrix, extra_matrix], axis=0)


def per_device(sigma_anc, panels, diag_inv, scaled_parent_panel, struct_upper, struct_lower):
    rows_grp, cols_dev = sigma_anc.shape
    rows_dev = panels.shape[0]
    grp_count = lax.axis_size("grp")
    blk_count = lax.axis_size("blk")
    grp_pos = lax.axis_index("grp")
    blk_pos = lax.axis_index("blk")
    blocks = cols_dev * blk_count // NODE_WIDTH
    table = block_table(struct_upper, struct_lower, blocks)
    parent_ids = jnp.arange(LOWER_NODES_2, dtype=jnp.int32) % UPPER_NODES_1
    membership_grid = (
        parent_ids[:, None] == jnp.arange(UPPER_NODES_1, dtype=jnp.int32)[None, :]
    ).astype(jnp.float32)
    stacked_arrays = scaled_parent_panel.reshape(LOWER_NODES_2, NODE_WIDTH, NODE_WIDTH)
    first_in = grp_pos * rows_grp + blk_pos * rows_dev
    upanel = panels * jnp.repeat(row_mask(table, first_in, rows_dev), NODE_WIDTH, axis=1)
    grouped = lax.all_gather(upanel, "blk", axis=0, tiled=True)
    partial_value = lax.dot_general(
        sigma_anc,
        grouped,
        (((0,), (0,)), ((), ())),
        precision=HIGH_ACCURACY,
        preferred_element_type=jnp.float32,
    )
    share = cols_dev // grp_count
    col_first = blk_pos * cols_dev
    root = col_first // rows_grp
    offset = jnp.clip(col_first - grp_pos * rows_grp, 0, rows_grp - cols_dev)
    own_first = col_first + grp_pos * share
    owned_mask = row_mask(table, own_first, share)
    nterms = UPPER_NODES_1 + 2 * LOWER_NODES_2
    inverse_columns = lax.psum(partial_value, "grp")
    inverse_owned = lax.dynamic_slice_in_dim(inverse_columns, grp_pos * share, share, 0)
    strip_result, collected_elder_share, resolved_bottom_share = strip_summands(
        inverse_owned, owned_mask, membership_grid, stacked_arrays
    )

    def on_root():
        u_cols = lax.dynamic_slice_in_dim(grouped, offset, cols_dev, 0)
        complete_mask = row_mask(table, col_first, cols_dev)
        discarded_result, collected_entire_factor, resolved_entire_factor = strip_summands(
            inverse_columns, complete_mask, membership_grid, stacked_arrays
        )
        return block_sums(u_cols, inverse_columns, collected_entire_factor, resolved_entire_factor)

    def off_root():
        return jnp.zeros((nterms, NODE_WIDTH, NODE_WIDTH), jnp.float32)

    terms = lax.cond(grp_pos == root, on_root, off_root)
    summed = lax.psum(terms, ("grp", "blk"))
    amat = summed[:UPPER_NODES_1]
    block_matrix = summed[UPPER_NODES_1 : UPPER_NODES_1 + LOWER_NODES_2]
    extra_matrix = summed[UPPER_NODES_1 + LOWER_NODES_2 :]
    diagonal_matrices = diag_inv.reshape(UPPER_NODES_1 + LOWER_NODES_2, NODE_WIDTH, NODE_WIDTH)
    s_up = diagonal_matrices[:UPPER_NODES_1] + amat
    parent_selection = jnp.einsum("cj,jwv->cwv", membership_grid, s_up, precision=HIGH_ACCURACY)
    solved_parent = jnp.einsum(
        "ghz,gzs->ghs", parent_selection, stacked_arrays, precision=HIGH_ACCURACY
    ) + jnp.transpose(block_matrix, (0, 2, 1))
    lower_selection = (
        diagonal_matrices[UPPER_NODES_1:]
        + jnp.einsum("lmt,lmx->ltx", stacked_arrays, solved_parent, precision=HIGH_ACCURACY)
        + extra_matrix
    )
    whole_diag = jnp.concatenate([s_up, lower_selection], axis=0).reshape(
        (UPPER_NODES_1 + LOWER_NODES_2) * NODE_WIDTH, NODE_WIDTH
    )
    whole_parent = -solved_parent.reshape(LOWER_NODES_2 * NODE_WIDTH, NODE_WIDTH)
    diag_rows = (UPPER_NODES_1 + LOWER_NODES_2) * NODE_WIDTH // blk_count
    parent_rows = LOWER_NODES_2 * NODE_WIDTH // blk_count
    cov_diag = lax.dynamic_slice_in_dim(whole_diag, blk_pos * diag_rows, diag_rows, 0)
    cov_parent = lax.dynamic_slice_in_dim(whole_parent, blk_pos * parent_rows, parent_rows, 0)
    return (strip_result, cov_diag, cov_parent)


def solution(mesh):
    return jax.shard_map(
        per_device,
        mesh=mesh,
        in_specs=(P("grp", "blk"), P(("grp", "blk"), None), P(), P(), P(), P()),
        out_specs=(P(("blk", "grp"), None), P("blk", None), P("blk", None)),
        check_vma=False,
    )
```

profile of v0, /device:TPU:17, one launch (start us, length us, event | category | flops | bytes accessed | tf_op | source)
XLA Modules:
  0.0 598.6 jit_solution(4750005704873806624)
XLA Ops:
  7.2 0.0 copy-start
  7.2 0.0 all-gather.2.cloned.1.call-start
  7.3 0.9 fusion.21
  8.2 0.8 fusion.22
  8.9 0.2 fusion.23
  9.1 0.1 broadcast_in_dim.7
  9.3 1.6 mul.37
  10.8 0.0 all-gather.2.cloned.1.call-update
  10.9 0.0 all-reduce.3.cloned.1.call-start
  10.9 74.6 %all-gather.2.cloned.1.call-done = f32[1024,1024]{1,0:T(8,128)} async-done(((f32[32,1024]{1,0:T(8,128)}), f32[1024,1024]{1,0:T(8,128)}) %all-gather.2.cloned.1.call-update) | async-done | bytes 4194320 | tf_op jit(solution)/shard_map/all_gather | solution.py:85
  85.5 0.0 copy-done
  85.5 9.6 %convolution_bitcast_fusion.2 = f32[512,1024]{0,1:T(8,128)} fusion(f32[1024,1024]{1,0:T(8,128)} %all-gather.2.cloned.1.call-done, f32[1024,512]{1,0:T(8,128)S(1)} %copy-done), kind=kOutput, calls=%fused_computation.24 | convolution fusion | flops 6442450944 | bytes 8388608 | tf_op jit(solution)/shard_map/dot_general | solution.py:86
  95.1 0.0 copy-start.8
  95.1 0.0 all-reduce.3.cloned.1.call-update
  95.2 0.0 all-reduce.5.cloned.1.call-start
  95.3 0.1 fusion.30
  95.3 1.0 copy-done.8
  96.4 1.1 fusion.35
  97.5 157.6 %all-reduce.3.cloned.1.call-done = f32[512,1024]{0,1:T(8,128)} async-done(((f32[512,1024]{0,1:T(8,128)}), f32[512,1024]{0,1:T(8,128)}) %all-reduce.3.cloned.1.call-update) | async-done | bytes 2097168 | tf_op jit(solution)/shard_map/psum | solution.py:100
  255.0 1.3 conditional.1
  255.0 1.3 broadcast.130
  256.4 0.0 copy-start.7
  256.4 3.1 copy.93
  259.4 0.0 copy-start.6
  259.4 0.0 all-reduce.5.cloned.1.call-update
  259.5 0.2 fusion.24
  259.7 0.0 copy-done.7
  259.7 1.0 copy.94
  260.7 0.0 copy-done.6
  260.7 1.0 copy.99
  261.7 0.0 copy-start.1
  261.7 1.3 fusion.19
  263.0 0.1 copy.91
  263.1 0.1 copy.86
  263.3 0.1 copy.88
  263.4 0.1 copy.89
  263.5 0.3 convolution_bitcast_fusion.4
  263.8 0.0 copy-done.1
  263.8 0.4 fusion.17
  264.2 0.7 pad_maximum_fusion.2
  264.9 313.5 %all-reduce.5.cloned.1.call-done = f32[6,256,256]{1,2,0:T(8,128)} async-done(((f32[6,256,256]{1,2,0:T(8,128)}), f32[6,256,256]{1,2,0:T(8,128)}) %all-reduce.5.cloned.1.call-update) | async-done | bytes 1572880 | tf_op jit(solution)/shard_map/psum | solution.py:118
  578.4 1.3 slice_add_fusion
  579.7 1.0 copy.95
  580.7 0.0 copy-start.5
  580.7 2.2 fusion.27
  582.9 2.5 fusion.36
  585.4 0.0 copy-done.5
  585.4 2.1 fusion.13
  587.5 1.0 pad_maximum_fusion.1
  588.5 1.6 copy.100
  590.1 0.6 constant_dynamic-slice_fusion.2
  590.7 1.3 constant_dynamic-slice_fusion.1
  (7 shorter events, 0.1 us)
Async XLA Ops:
  7.2 78.4 %copy-start = (f32[1024,512]{1,0:T(8,128)S(1)}, f32[1024,512]{1,0:T(8,128)}, u32[]{:S(2)}) copy-start(f32[1024,512]{1,0:T(8,128)} %param.8) | copy-start | bytes 6291460
  7.2 78.3 %all-gather.2.cloned.1.call-start = ((), (), s32[]{:S(2)}) async-start(), calls=%async_computation | async-start | bytes 4325376 | tf_op jit(solution)/shard_map/all_gather | solution.py:85
  10.9 244.2 %all-reduce.3.cloned.1.call-start = ((), (), s32[]{:S(2)}) async-start(), calls=%async_computation.1 | async-start | bytes 4194304 | tf_op jit(solution)/shard_map/psum | solution.py:100
  95.1 1.2 copy-start.8
  95.2 483.3 %all-reduce.5.cloned.1.call-start = ((), (), s32[]{:S(2)}) async-start(), calls=%async_computation.2 | async-start | bytes 3145728 | tf_op jit(solution)/shard_map/psum | solution.py:118
  256.4 3.3 copy-start.7
  259.4 1.2 copy-start.6
  261.7 2.1 copy-start.1
  580.7 4.7 copy-start.5
Sparse Core Ops, SparseCore 0:
  11.0 74.4 all-gather.1
  95.3 159.7 all-reduce.2
  259.9 318.4 all-reduce.4
where the time goes:
time: 599 us
  waiting for transfers between devices  546 us (91%)
  matrix products  17.5 us (3%)
  between operations  13.9 us (2%)
  local copies, waits for them, and re-layouts  13.7 us (2%)
  other arithmetic  7.63 us (1%)
    psum x1, waiting for transfers between devices, per_device(): summed = lax.psum(terms, ('grp', 'blk'))  314 us
    psum x1, waiting for transfers between devices, per_device(): inverse_columns = lax.psum(partial_value, 'grp')  158 us
    all_gather x1, waiting for transfers between devices, per_device(): grouped = lax.all_gather(upanel, 'blk', axis=0, tiled=True)  74.6 us
  transfers between devices with their start and end apart: 3, of which 3 were waited for; matrix products, arithmetic and copies ran while one was open for 1% of the time, Pallas kernels for 0%

commit v1 on v0

--- a/solution.py
+++ b/solution.py
@@ -82,7 +82,8 @@
     stacked_arrays = scaled_parent_panel.reshape(LOWER_NODES_2, NODE_WIDTH, NODE_WIDTH)
     first_in = grp_pos * rows_grp + blk_pos * rows_dev
     upanel = panels * jnp.repeat(row_mask(table, first_in, rows_dev), NODE_WIDTH, axis=1)
-    grouped = lax.all_gather(upanel, "blk", axis=0, tiled=True)
+    stack = jnp.stack([upanel] * lax.axis_size("blk"))
+    grouped = jnp.concatenate(lax.all_to_all(stack, "blk", 0, 0), axis=0)
     partial_value = lax.dot_general(
         sigma_anc,
         grouped,

time: 599 us -> 631 us (1.053)
  blocking collectives: 0 us -> 106 us
  waiting for transfers between devices: 546 us -> 471 us
    all_to_all x0 -> x1, blocking collectives: none -> 106 us  [per_device(): grouped = jnp.concatenate(lax.all_to_all(stack, 'blk', 0, 0), axis=0)]
    all_gather x1 -> x0, waiting for transfers between devices: 74.6 us -> none  [per_device(): grouped = lax.all_gather(upanel, 'blk', axis=0, tiled=True)]
  transfers between devices with their start and end apart: 3 -> 2, of which waited for: 3 -> 2; matrix products, arithmetic and copies ran while one was open for 1% -> 1% of each run, Pallas kernels for 0% -> 0%
where the time goes in v1:
time: 631 us; the launch traced here: 630 us
  waiting for transfers between devices  471 us (75%)
  blocking collectives  106 us (17%)
  local copies, waits for them, and re-layouts  16.1 us (3%)
  matrix products  16 us (3%)
  between operations  14.2 us (2%)
  other arithmetic  6.97 us (1%)
    psum x1, waiting for transfers between devices, per_device(): summed = lax.psum(terms, ('grp', 'blk'))  313 us
    psum x1, waiting for transfers between devices, per_device(): inverse_columns = lax.psum(partial_value, 'grp')  157 us
    all_to_all x1, blocking collectives, per_device(): grouped = jnp.concatenate(lax.all_to_all(stack, 'blk', 0, 0), axis=0)  106 us
  transfers between devices with their start and end apart: 2, of which 2 were waited for; matrix products, arithmetic and copies ran while one was open for 1% of the time, Pallas kernels for 0%

profile of v1, /device:TPU:17, one launch (start us, length us, event | category | flops | bytes accessed | tf_op | source)
XLA Modules:
  0.0 630.0 jit_solution(12287573798359658634)
XLA Ops:
  7.2 0.0 copy-start
  7.2 0.0 all-reduce.3.cloned.1.call-start
  7.3 0.9 fusion.21
  8.2 0.8 fusion.22
  8.9 0.2 fusion.23
  9.1 0.1 broadcast_in_dim.7
  9.3 0.9 mul.37
  10.2 0.5 stack.2
  10.7 105.8 %all_to_all.5 = f32[32,32,1024]{2,1,0:T(8,128)S(1)} all-to-all(f32[32,32,1024]{2,1,0:T(8,128)S(1)} %stack.2), channel_id=1, replica_groups=mesh['grp'=16,'blk'=32] {'blk'}, dimensions={0} | all-to-all | bytes 8388608 | tf_op jit(solution)/shard_map/all_to_all | solution.py:86
  116.5 0.0 copy-start.1
  116.5 2.0 copy-done.1
  118.5 0.0 copy-done
  118.5 8.1 %convolution_bitcast_fusion.2 = f32[512,1024]{0,1:T(8,128)} fusion(f32[1024,1024]{1,0:T(8,128)S(1)} %bitcast.78, f32[1024,512]{1,0:T(8,128)S(1)} %copy-done), kind=kOutput, calls=%fused_computation.24 | convolution fusion | flops 6442450944 | bytes 8388608 | tf_op jit(solution)/shard_map/dot_general | solution.py:87
  126.6 0.0 copy-start.9
  126.6 0.0 all-reduce.3.cloned.1.call-update
  126.6 0.0 all-reduce.5.cloned.1.call-start
  126.7 0.1 fusion.30
  126.8 1.0 copy-done.9
  127.8 1.1 fusion.35
  128.9 157.3 %all-reduce.3.cloned.1.call-done = f32[512,1024]{0,1:T(8,128)} async-done(((f32[512,1024]{0,1:T(8,128)}), f32[512,1024]{0,1:T(8,128)}) %all-reduce.3.cloned.1.call-update) | async-done | bytes 2097168 | tf_op jit(solution)/shard_map/psum | solution.py:101
  286.2 1.3 conditional.1
  286.2 1.3 broadcast.132
  287.5 0.0 copy-start.8
  287.5 3.1 copy.95
  290.6 0.0 copy-start.7
  290.6 0.0 all-reduce.5.cloned.1.call-update
  290.7 0.2 fusion.24
  290.8 0.0 copy-done.8
  290.8 1.0 copy.96
  291.9 0.0 copy-done.7
  291.9 1.0 copy.101
  292.9 0.0 copy-start.2
  292.9 1.3 fusion.19
  294.2 0.1 copy.93
  294.3 0.1 copy.88
  294.4 0.1 copy.90
  294.6 0.1 copy.91
  294.7 0.3 convolution_bitcast_fusion.4
  295.0 0.0 copy-done.2
  295.0 0.4 fusion.17
  295.4 0.7 pad_maximum_fusion.2
  296.1 313.5 %all-reduce.5.cloned.1.call-done = f32[6,256,256]{1,2,0:T(8,128)} async-done(((f32[6,256,256]{1,2,0:T(8,128)}), f32[6,256,256]{1,2,0:T(8,128)}) %all-reduce.5.cloned.1.call-update) | async-done | bytes 1572880 | tf_op jit(solution)/shard_map/psum | solution.py:119
  609.6 1.3 slice_add_fusion
  610.8 1.0 copy.97
  611.8 0.0 copy-start.6
  611.8 2.2 fusion.27
  614.0 2.5 fusion.36
  616.5 0.0 copy-done.6
  616.5 2.1 fusion.13
  618.6 1.0 pad_maximum_fusion.1
  619.7 1.6 copy.102
  621.2 0.6 constant_dynamic-slice_fusion.2
  621.8 1.3 constant_dynamic-slice_fusion.1
  (7 shorter events, 0.1 us)
Async XLA Ops:
  7.2 111.3 %copy-start = (f32[1024,512]{1,0:T(8,128)S(1)}, f32[1024,512]{1,0:T(8,128)}, u32[]{:S(2)}) copy-start(f32[1024,512]{1,0:T(8,128)} %param.8) | copy-start | bytes 6291460
  7.2 279.0 %all-reduce.3.cloned.1.call-start = ((), (), s32[]{:S(2)}) async-start(), calls=%async_computation.1 | async-start | bytes 4194304 | tf_op jit(solution)/shard_map/psum | solution.py:101
  116.5 2.0 copy-start.1
  126.6 1.2 copy-start.9
  126.6 483.0 %all-reduce.5.cloned.1.call-start = ((), (), s32[]{:S(2)}) async-start(), calls=%async_computation.2 | async-start | bytes 3145728 | tf_op jit(solution)/shard_map/psum | solution.py:119
  287.5 3.3 copy-start.8
  290.6 1.2 copy-start.7
  292.9 2.1 copy-start.2
  611.8 4.7 copy-start.6
Sparse Core Ops, SparseCore 0:
  126.7 159.4 all-reduce.2
  291.1 318.3 all-reduce.4
